TPU v7x, 512 devices: a whole 4x8x8 slice. The times are simulated.
512 devices in a mesh: row: 16 (over z, core), col: 32 (over x, y).
Axes of the slice: x: 4, y: 8, z: 8, core: 2. Of those that a mesh axis runs over, the one named last changes fastest.
Arguments:
- panels: float32 [8192, 16384], P('row', 'col'), as said below
Outputs:
- r_rows: float32 [256, 16384], P(None, 'col')
Inputs may be any that keep to these rules, and one draw needn't show every extreme that they name: `panels`: the first 256 columns of W have full column rank.
All inputs are finite; a program needn't handle non-finite values.
Results may differ from a plain program's by a relative error of at most 0.0003.
Values sent between devices are 32-bit elements; how exact they have to be, the bound alone decides.
A program may use at most 64 MiB of HBM per device.

v0:
```python
import jax
import jax.numpy as jnp
from jax import lax
from jax.sharding import PartitionSpec as P

PANEL = 128


def swapped(shard, axis, distance):
    return lax.ppermute(shard, axis, [(i, i ^ 1 << distance) for i in range(lax.axis_size(axis))])


def spread_2(block, axis, source):
    block = jnp.where(lax.axis_index(axis) == source, block, jnp.zeros_like(block))
    return lax.psum(block, axis)


def matmul(left, right):
    return jnp.dot(left, right, precision=lax.Precision.HIGHEST, preferred_element_type=jnp.float32)


def contract_rows(left, right):
    return lax.dot_general(
        left,
        right,
        (((0,), (0,)), ((), ())),
        precision=lax.Precision.HIGHEST,
        preferred_element_type=jnp.float32,
    )


def outer_rows(left, right):
    return lax.dot_general(
        left,
        right,
        (((1,), (1,)), ((), ())),
        precision=lax.Precision.HIGHEST,
        preferred_element_type=jnp.float32,
    )


def factor(columns):
    first_low = jnp.linalg.cholesky(contract_rows(columns, columns))
    basis_one = jax.scipy.linalg.solve_triangular(first_low, columns.T, lower=True)
    second_low = jnp.linalg.cholesky(outer_rows(basis_one, basis_one))
    basis_t = jax.scipy.linalg.solve_triangular(second_low, basis_one, lower=True)
    triangle = matmul(first_low, second_low).T
    return (basis_t, triangle)


def lower_side(level_bit):
    return lax.axis_index("row") >> level_bit & 1 == 0


def stack_pair(mine, other, is_lower):
    return jnp.concatenate(
        [jnp.where(is_lower, mine, other), jnp.where(is_lower, other, mine)], axis=0
    )


def own_half(level_basis, is_lower):
    start = jnp.where(is_lower, 0, PANEL).astype(jnp.int32)
    return lax.dynamic_slice_in_dim(level_basis, start, PANEL, 1)


def spread_back(halves, top_rows, basis_t, working):
    spread = top_rows
    for my_half in reversed(halves):
        spread = contract_rows(my_half, spread)
    return working - contract_rows(basis_t, spread)


def owner_step(working, panels, panel_index):
    depth_count = lax.axis_size("row").bit_length() - 1
    is_owner = lax.axis_index("col") == panel_index
    columns = jnp.where(is_owner, working[:, :PANEL], panels[:, :PANEL])
    basis_t, triangle = factor(columns)
    level_list = []
    for level_bit in range(depth_count):
        other_tri = swapped(triangle, "row", level_bit)
        level_basis, triangle = factor(stack_pair(triangle, other_tri, lower_side(level_bit)))
        level_list.append(level_basis)
    basis_t, level_stack = (
        spread_2(basis_t, "col", panel_index),
        spread_2(jnp.stack(level_list), "col", panel_index),
    )
    top_rows = matmul(basis_t, working)
    halves = []
    for level_bit in range(depth_count):
        other_top = swapped(top_rows, "row", level_bit)
        is_lower = lower_side(level_bit)
        top_rows = matmul(level_stack[level_bit], stack_pair(top_rows, other_top, is_lower))
        halves.append(own_half(level_stack[level_bit], is_lower))
    return (top_rows, spread_back(halves, top_rows, basis_t, working))


def local(panels):
    working = panels
    pieces = []
    for panel_index in range(2):
        top_rows, working = owner_step(working, panels, panel_index)
        pieces.append(top_rows)
    top_block = jnp.concatenate(pieces, axis=0)
    local_width = panels.shape[1]
    col_iota = jnp.arange(local_width, dtype=jnp.int32)
    global_col = (
        col_iota // PANEL * lax.axis_size("col") + lax.axis_index("col")
    ) * PANEL + col_iota % PANEL
    row_iota = jnp.arange(2 * PANEL, dtype=jnp.int32)
    keep_mask = global_col[None, :] >= row_iota[:, None]
    return jnp.where(keep_mask, top_block, jnp.zeros_like(top_block))


def solution(mesh):
    return jax.shard_map(
        local, mesh=mesh, in_specs=(P("row", "col"),), out_specs=P(None, "col"), check_vma=False
    )
```

profile of v0, /device:TPU:1, one launch (start us, length us, event | category | flops | bytes accessed | tf_op | source)
XLA Modules:
  0.0 1003.0 jit_solution(15096186413171939091)
XLA Ops:
  8.3 11.7 %cholesky.314 = f32[128,128]{1,0:T(8,128)S(1)} custom-call(f32[128,128]{1,0:T(8,128)S(1)} %fusion.119), custom_call_target="Cholesky" | custom-call | tf_op jit(solution)/shard_map/jit(cholesky)/cholesky | solution.py:43
  21.3 9.8 custom-call.26
  33.0 11.7 %cholesky.325 = f32[128,128]{1,0:T(8,128)S(1)} custom-call(f32[128,128]{1,0:T(8,128)S(1)} %fusion.117), custom_call_target="Cholesky" | custom-call | tf_op jit(solution)/shard_map/jit(cholesky)/cholesky | solution.py:45
  47.1 9.0 collective-permute-start
  56.9 9.8 custom-call.35
  68.3 11.7 %cholesky.336 = f32[128,128]{1,0:T(8,128)S(1)} custom-call(f32[128,128]{1,0:T(8,128)S(1)} %fusion.116), custom_call_target="Cholesky" | custom-call | tf_op jit(solution)/shard_map/jit(cholesky)/cholesky | solution.py:43
  81.4 9.8 custom-call.27
  91.9 22.8 %cholesky.347 = f32[128,128]{1,0:T(8,128)S(1)} custom-call(f32[128,128]{1,0:T(8,128)S(1)} %fusion.114), custom_call_target="Cholesky" | custom-call | tf_op jit(solution)/shard_map/jit(cholesky)/cholesky | solution.py:45
  117.8 9.8 custom-call.28
  129.8 3.3 collective-permute-done.1
  133.6 11.7 %cholesky.358 = f32[128,128]{1,0:T(8,128)S(1)} custom-call(f32[128,128]{1,0:T(8,128)S(1)} %fusion.112), custom_call_target="Cholesky" | custom-call | tf_op jit(solution)/shard_map/jit(cholesky)/cholesky | solution.py:43
  146.7 9.8 custom-call.29
  157.2 11.7 %cholesky.369 = f32[128,128]{1,0:T(8,128)S(1)} custom-call(f32[128,128]{1,0:T(8,128)S(1)} %fusion.110), custom_call_target="Cholesky" | custom-call | tf_op jit(solution)/shard_map/jit(cholesky)/cholesky | solution.py:45
  172.0 10.2 %custom-call.30 = f32[1,128,128]{1,2,0:T(8,128)S(1)} custom-call(f32[1,128,128]{2,1,0:T(8,128)S(1)} %select_bitcast_fusion.11), custom_call_target="InvertDiagBlocksLowerTriangular" | custom-call | tf_op jit(solution)/shard_map/jit(_solve_triangular)/triangular_solve | solution.py:46
  184.5 5.7 collective-permute-done.2
  190.7 11.7 %cholesky.380 = f32[128,128]{1,0:T(8,128)S(1)} custom-call(f32[128,128]{1,0:T(8,128)S(1)} %fusion.108), custom_call_target="Cholesky" | custom-call | tf_op jit(solution)/shard_map/jit(cholesky)/cholesky | solution.py:43
  203.8 9.8 custom-call.31
  214.3 11.7 %cholesky.391 = f32[128,128]{1,0:T(8,128)S(1)} custom-call(f32[128,128]{1,0:T(8,128)S(1)} %fusion.106), custom_call_target="Cholesky" | custom-call | tf_op jit(solution)/shard_map/jit(cholesky)/cholesky | solution.py:45
  229.1 10.0 custom-call.32
  242.6 5.3 collective-permute-done.3
  248.5 11.7 %cholesky.402 = f32[128,128]{1,0:T(8,128)S(1)} custom-call(f32[128,128]{1,0:T(8,128)S(1)} %fusion.104), custom_call_target="Cholesky" | custom-call | tf_op jit(solution)/shard_map/jit(cholesky)/cholesky | solution.py:43
  261.6 9.8 custom-call.33
  272.1 11.7 %cholesky.413 = f32[128,128]{1,0:T(8,128)S(1)} custom-call(f32[128,128]{1,0:T(8,128)S(1)} %fusion.102), custom_call_target="Cholesky" | custom-call | tf_op jit(solution)/shard_map/jit(cholesky)/cholesky | solution.py:45
  285.1 10.2 %custom-call.34 = f32[1,128,128]{1,2,0:T(8,128)S(1)} custom-call(f32[1,128,128]{2,1,0:T(8,128)S(1)} %fusion.69), custom_call_target="InvertDiagBlocksLowerTriangular" | custom-call | tf_op jit(solution)/shard_map/jit(_solve_triangular)/triangular_solve | solution.py:46
  296.6 156.7 %all-reduce.7.cloned.1.call-done = (f32[128,512]{1,0:T(8,128)}, f32[4,128,256]{2,1,0:T(8,128)}) async-done(((f32[128,512]{1,0:T(8,128)}, f32[4,128,256]{2,1,0:T(8,128)}), (f32[128,512]{1,0:T(8,128)}, f32[4,128,256]{2,1,0:T(8,128)})) %all-reduce.7.cloned.1.call-update) | async-done | bytes 786448 | tf_op jit(solution)/shard_map/psum | solution.py:15
  454.9 7.5 collective-permute-start.4
  464.0 3.3 collective-permute-start.5
  467.3 6.1 collective-permute-done.5
  473.9 4.4 collective-permute-start.6
  478.3 11.3 %collective-permute-done.6 = f32[128,512]{1,0:T(8,128)S(1)} collective-permute-done((f32[128,512]{1,0:T(8,128)S(1)}, f32[128,512]{1,0:T(8,128)S(1)}, u32[]{:S(2)}, u32[]{:S(2)}) %collective-permute-start.6) | collective-permute-done | bytes 262176 | tf_op jit(solution)/shard_map/ppermute | solution.py:10
  490.0 8.5 collective-permute-start.7
  498.6 11.5 %collective-permute-done.7 = f32[128,512]{1,0:T(8,128)S(1)} collective-permute-done((f32[128,512]{1,0:T(8,128)S(1)}, f32[128,512]{1,0:T(8,128)S(1)}, u32[]{:S(2)}, u32[]{:S(2)}) %collective-permute-start.7) | collective-permute-done | bytes 262176 | tf_op jit(solution)/shard_map/ppermute | solution.py:10
  514.7 11.7 %cholesky.424 = f32[128,128]{1,0:T(8,128)S(1)} custom-call(f32[128,128]{1,0:T(8,128)S(1)} %fusion.91), custom_call_target="Cholesky" | custom-call | tf_op jit(solution)/shard_map/jit(cholesky)/cholesky | solution.py:43
  527.8 9.8 custom-call.36
  538.5 11.9 %cholesky.435 = f32[128,128]{1,0:T(8,128)S(1)} custom-call(f32[128,128]{1,0:T(8,128)S(1)} %fusion.89), custom_call_target="Cholesky" | custom-call | tf_op jit(solution)/shard_map/jit(cholesky)/cholesky | solution.py:45
  556.7 9.8 custom-call.45
  568.2 11.7 %cholesky.446 = f32[128,128]{1,0:T(8,128)S(1)} custom-call(f32[128,128]{1,0:T(8,128)S(1)} %fusion.88), custom_call_target="Cholesky" | custom-call | tf_op jit(solution)/shard_map/jit(cholesky)/cholesky | solution.py:43
  581.3 9.8 custom-call.37
  591.8 12.1 %cholesky.457 = f32[128,128]{1,0:T(8,128)S(1)} custom-call(f32[128,128]{1,0:T(8,128)S(1)} %fusion.86), custom_call_target="Cholesky" | custom-call | tf_op jit(solution)/shard_map/jit(cholesky)/cholesky | solution.py:45
  607.0 9.8 custom-call.38
  619.0 3.3 collective-permute-done.9
  622.8 11.7 %cholesky.468 = f32[128,128]{1,0:T(8,128)S(1)} custom-call(f32[128,128]{1,0:T(8,128)S(1)} %fusion.84), custom_call_target="Cholesky" | custom-call | tf_op jit(solution)/shard_map/jit(cholesky)/cholesky | solution.py:43
  635.9 9.8 custom-call.39
  646.4 11.7 %cholesky.479 = f32[128,128]{1,0:T(8,128)S(1)} custom-call(f32[128,128]{1,0:T(8,128)S(1)} %fusion.82), custom_call_target="Cholesky" | custom-call | tf_op jit(solution)/shard_map/jit(cholesky)/cholesky | solution.py:45
  661.2 10.0 custom-call.40
  671.2 3.5 collective-permute-start.10
  675.0 4.0 collective-permute-done.10
  679.5 11.7 %cholesky.490 = f32[128,128]{1,0:T(8,128)S(1)} custom-call(f32[128,128]{1,0:T(8,128)S(1)} %fusion.80), custom_call_target="Cholesky" | custom-call | tf_op jit(solution)/shard_map/jit(cholesky)/cholesky | solution.py:43
  692.5 9.8 custom-call.41
  703.1 11.7 %cholesky.501 = f32[128,128]{1,0:T(8,128)S(1)} custom-call(f32[128,128]{1,0:T(8,128)S(1)} %fusion.78), custom_call_target="Cholesky" | custom-call | tf_op jit(solution)/shard_map/jit(cholesky)/cholesky | solution.py:45
  717.9 10.0 custom-call.42
  727.9 4.4 collective-permute-start.11
  732.6 5.2 collective-permute-done.11
  738.4 11.7 %cholesky.512 = f32[128,128]{1,0:T(8,128)S(1)} custom-call(f32[128,128]{1,0:T(8,128)S(1)} %fusion.76), custom_call_target="Cholesky" | custom-call | tf_op jit(solution)/shard_map/jit(cholesky)/cholesky | solution.py:43
  751.4 9.8 custom-call.43
  761.9 11.7 %cholesky.523 = f32[128,128]{1,0:T(8,128)S(1)} custom-call(f32[128,128]{1,0:T(8,128)S(1)} %fusion.74), custom_call_target="Cholesky" | custom-call | tf_op jit(solution)/shard_map/jit(cholesky)/cholesky | solution.py:45
  775.0 10.0 custom-call.44
  786.2 151.2 %all-reduce.5.cloned.1.call-done = (f32[128,512]{1,0:T(8,128)}, f32[4,128,256]{2,1,0:T(8,128)}) async-done(((f32[128,512]{1,0:T(8,128)}, f32[4,128,256]{2,1,0:T(8,128)}), (f32[128,512]{1,0:T(8,128)}, f32[4,128,256]{2,1,0:T(8,128)})) %all-reduce.5.cloned.1.call-update) | async-done | bytes 786448 | tf_op jit(solution)/shard_map/psum | solution.py:15
  939.1 7.5 collective-permute-start.12
  951.5 6.1 collective-permute-done.13
  958.1 4.4 collective-permute-start.14
  962.5 11.3 %collective-permute-done.14 = f32[128,512]{1,0:T(8,128)S(1)} collective-permute-done((f32[128,512]{1,0:T(8,128)S(1)}, f32[128,512]{1,0:T(8,128)S(1)}, u32[]{:S(2)}, u32[]{:S(2)}) %collective-permute-start.14) | collective-permute-done | bytes 262176 | tf_op jit(solution)/shard_map/ppermute | solution.py:10
  974.2 8.5 collective-permute-start.15
  982.8 11.6 %collective-permute-done.15 = f32[128,512]{1,0:T(8,128)S(1)} collective-permute-done((f32[128,512]{1,0:T(8,128)S(1)}, f32[128,512]{1,0:T(8,128)S(1)}, u32[]{:S(2)}, u32[]{:S(2)}) %collective-permute-start.15) | collective-permute-done | bytes 262176 | tf_op jit(solution)/shard_map/ppermute | solution.py:10
  (206 shorter events, 90.9 us)
Async XLA Ops:
  6.5 446.7 %all-reduce.7.cloned.1.call-start = ((), (), s32[]{:S(2)}) async-start(), calls=%async_computation.1 | async-start | bytes 1572864 | tf_op jit(solution)/shard_map/psum | solution.py:15
  47.1 20.7 %collective-permute-start = (f32[128,128]{1,0:T(8,128)S(1)}, f32[128,128]{1,0:T(8,128)S(1)}, u32[]{:S(2)}, u32[]{:S(2)}) collective-permute-start(f32[128,128]{1,0:T(8,128)S(1)} %fusion.141), channel_id=1, source_target_pairs={{0,32},{32,0},{64,96},{96,64},{128,160},{160,128},{192,224},{224,1... | collective-permute-start | bytes 196616 | tf_op jit(solution)/shard_map/ppermute | solution.py:10
  127.6 5.5 collective-permute-start.1
  182.2 7.9 collective-permute-start.2
  239.1 8.9 collective-permute-start.3
  295.3 157.9 %copy-start = (f32[512,512]{1,0:T(8,128)S(1)}, f32[512,512]{1,0:T(8,128)}, u32[]{:S(2)}) copy-start(f32[512,512]{1,0:T(8,128)} %param.6) | copy-start | bytes 3145732
  296.5 640.9 %all-reduce.5.cloned.1.call-start = ((), (), s32[]{:S(2)}) async-start(), calls=%async_computation | async-start | bytes 1572864 | tf_op jit(solution)/shard_map/psum | solution.py:15
  454.9 8.7 copy-start.1
  454.9 8.6 collective-permute-start.4
  464.0 9.4 collective-permute-start.5
  473.9 15.7 %collective-permute-start.6 = (f32[128,512]{1,0:T(8,128)S(1)}, f32[128,512]{1,0:T(8,128)S(1)}, u32[]{:S(2)}, u32[]{:S(2)}) collective-permute-start(f32[128,512]{1,0:T(8,128)S(1)} %fusion.4), channel_id=1, source_target_pairs={{0,128},{32,160},{64,192},{96,224},{128,0},{160,32},{192,64},{224,... | collective-permute-start | bytes 786440 | tf_op jit(solution)/shard_map/ppermute | solution.py:10
  490.0 20.1 %collective-permute-start.7 = (f32[128,512]{1,0:T(8,128)S(1)}, f32[128,512]{1,0:T(8,128)S(1)}, u32[]{:S(2)}, u32[]{:S(2)}) collective-permute-start(f32[128,512]{1,0:T(8,128)S(1)} %fusion.8), channel_id=1, source_target_pairs={{0,256},{32,288},{64,320},{96,352},{128,384},{160,416},{192,448},{... | collective-permute-start | bytes 786440 | tf_op jit(solution)/shard_map/ppermute | solution.py:10
  512.0 1.0 copy-start.2
  553.5 14.2 %collective-permute-start.8 = (f32[128,128]{1,0:T(8,128)S(1)}, f32[128,128]{1,0:T(8,128)S(1)}, u32[]{:S(2)}, u32[]{:S(2)}) collective-permute-start(f32[128,128]{1,0:T(8,128)S(1)} %fusion.146), channel_id=1, source_target_pairs={{0,32},{32,0},{64,96},{96,64},{128,160},{160,128},{192,224},{224,1... | collective-permute-start | bytes 196616 | tf_op jit(solution)/shard_map/ppermute | solution.py:10
  616.8 5.5 collective-permute-start.9
  671.2 7.8 collective-permute-start.10
  727.9 9.9 collective-permute-start.11
  939.1 8.7 copy-start.3
  939.1 8.6 collective-permute-start.12
  948.2 9.4 collective-permute-start.13
  958.1 15.7 %collective-permute-start.14 = (f32[128,512]{1,0:T(8,128)S(1)}, f32[128,512]{1,0:T(8,128)S(1)}, u32[]{:S(2)}, u32[]{:S(2)}) collective-permute-start(f32[128,512]{1,0:T(8,128)S(1)} %fusion.20), channel_id=1, source_target_pairs={{0,128},{32,160},{64,192},{96,224},{128,0},{160,32},{192,64},{224,... | collective-permute-start | bytes 786440 | tf_op jit(solution)/shard_map/ppermute | solution.py:10
  974.2 20.1 %collective-permute-start.15 = (f32[128,512]{1,0:T(8,128)S(1)}, f32[128,512]{1,0:T(8,128)S(1)}, u32[]{:S(2)}, u32[]{:S(2)}) collective-permute-start(f32[128,512]{1,0:T(8,128)S(1)} %fusion.24), channel_id=1, source_target_pairs={{0,256},{32,288},{64,320},{96,352},{128,384},{160,416},{192,448},{... | collective-permute-start | bytes 786440 | tf_op jit(solution)/shard_map/ppermute | solution.py:10
Sparse Core Ops, SparseCore 0:
  296.6 156.5 all-reduce.6
  786.3 151.0 all-reduce.4
where the time goes:
time: 1010 us; the launch traced here: 1000 us
  other arithmetic  474 us (47%)
  waiting for transfers between devices  395 us (39%)
  starting transfers between devices  76.4 us (8%)
  matrix products  39.8 us (4%)
  between operations  15.2 us (2%)
    psum x2, waiting for transfers between devices, spread_2(): return lax.psum(block, axis)  308 us
    another operation x30, other arithmetic, factor(): second_low = jnp.linalg.cholesky(outer_rows(basis_one, basis_one))  136 us
    another operation x30, other arithmetic, factor(): first_low = jnp.linalg.cholesky(contract_rows(columns, columns))  124 us
    another operation x20, other arithmetic, factor(): jax.scipy.linalg.solve_triangular(second_low, basis_one, lower=True)  106 us
    another operation x20, other arithmetic, factor(): jax.scipy.linalg.solve_triangular(first_low, columns.T, lower=True)  105 us
    ppermute x16, waiting for transfers between devices, swapped(): lax.ppermute(shard, axis, [(i, i ^ 1 << distance) for i in range(lax.axis...  87 us
    ppermute x16, starting transfers between devices, swapped(): lax.ppermute(shard, axis, [(i, i ^ 1 << distance) for i in range(lax.axis...  76.3 us
  transfers between devices with their start and end apart: 18, of which 16 were waited for; matrix products, arithmetic and copies ran while one was open for 2% of the time, Pallas kernels for 0%

commit v1 on v0

--- a/solution.py
+++ b/solution.py
@@ -12,7 +12,7 @@
 
 def spread_2(block, axis, source):
     block = jnp.where(lax.axis_index(axis) == source, block, jnp.zeros_like(block))
-    return lax.psum(block, axis)
+    return jnp.sum(lax.all_gather(block, axis), axis=0)
 
 
 def matmul(left, right):

time: 1010 us -> 979 us (0.969)
  waiting for transfers between devices: 395 us -> 348 us
  other arithmetic: 474 us -> 495 us
    psum x2 -> x0, waiting for transfers between devices: 308 us -> none  [spread_2(): return lax.psum(block, axis)]
    all_gather x0 -> x4, waiting for transfers between devices: none -> 264 us  [spread_2(): return jnp.sum(lax.all_gather(block, axis), axis=0)]
    reduce_sum x0 -> x4, other arithmetic: none -> 22.4 us  [spread_2(): return jnp.sum(lax.all_gather(block, axis), axis=0)]
    another operation x30, other arithmetic: 136 us -> 125 us  [factor(): second_low = jnp.linalg.cholesky(outer_rows(basis_one, basis_one))]
  transfers between devices with their start and end apart: 18 -> 20, of which waited for: 16 -> 18; matrix products, arithmetic and copies ran while one was open for 2% -> 43% of each run, Pallas kernels for 0% -> 0%
where the time goes in v1:
time: 979 us; the launch traced here: 969 us
  other arithmetic  495 us (51%)
  waiting for transfers between devices  348 us (36%)
  starting transfers between devices  71.6 us (7%)
  matrix products  37.9 us (4%)
  between operations  14.9 us (2%)
    all_gather x4, waiting for transfers between devices, spread_2(): return jnp.sum(lax.all_gather(block, axis), axis=0)  264 us
    another operation x30, other arithmetic, factor(): second_low = jnp.linalg.cholesky(outer_rows(basis_one, basis_one))  125 us
    another operation x30, other arithmetic, factor(): first_low = jnp.linalg.cholesky(contract_rows(columns, columns))  124 us
    another operation x20, other arithmetic, factor(): jax.scipy.linalg.solve_triangular(second_low, basis_one, lower=True)  116 us
    another operation x20, other arithmetic, factor(): jax.scipy.linalg.solve_triangular(first_low, columns.T, lower=True)  105 us
    ppermute x16, waiting for transfers between devices, swapped(): lax.ppermute(shard, axis, [(i, i ^ 1 << distance) for i in range(lax.axis...  83.4 us
    ppermute x16, starting transfers between devices, swapped(): lax.ppermute(shard, axis, [(i, i ^ 1 << distance) for i in range(lax.axis...  71.5 us
    reduce_sum x4, other arithmetic, spread_2(): return jnp.sum(lax.all_gather(block, axis), axis=0)  22.4 us
  transfers between devices with their start and end apart: 20, of which 18 were waited for; matrix products, arithmetic and copies ran while one was open for 43% of the time, Pallas kernels for 0%

profile of v1, /device:TPU:1, one launch (start us, length us, event | category | flops | bytes accessed | tf_op | source)
XLA Modules:
  0.0 969.5 jit_solution(16762615499997640943)
XLA Ops:
  8.4 11.7 %cholesky.314 = f32[128,128]{1,0:T(8,128)S(1)} custom-call(f32[128,128]{1,0:T(8,128)S(1)} %fusion.119), custom_call_target="Cholesky" | custom-call | tf_op jit(solution)/shard_map/jit(cholesky)/cholesky | solution.py:43
  21.4 9.8 %custom-call.26 = f32[1,128,128]{1,2,0:T(8,128)S(1)} custom-call(f32[1,128,128]{2,1,0:T(8,128)S(1)} %fusion.127), custom_call_target="InvertDiagBlocksLowerTriangular" | custom-call | tf_op jit(solution)/shard_map/jit(_solve_triangular)/triangular_solve | solution.py:44
  33.1 11.7 %cholesky.325 = f32[128,128]{1,0:T(8,128)S(1)} custom-call(f32[128,128]{1,0:T(8,128)S(1)} %fusion.117), custom_call_target="Cholesky" | custom-call | tf_op jit(solution)/shard_map/jit(cholesky)/cholesky | solution.py:45
  46.3 10.0 %custom-call.35 = f32[1,128,128]{1,2,0:T(8,128)S(1)} custom-call(f32[1,128,128]{2,1,0:T(8,128)S(1)} %select_bitcast_fusion.8), custom_call_target="InvertDiagBlocksLowerTriangular" | custom-call | tf_op jit(solution)/shard_map/jit(_solve_triangular)/triangular_solve | solution.py:46
  59.2 8.8 collective-permute-start
  69.3 11.7 %cholesky.336 = f32[128,128]{1,0:T(8,128)S(1)} custom-call(f32[128,128]{1,0:T(8,128)S(1)} %fusion.116), custom_call_target="Cholesky" | custom-call | tf_op jit(solution)/shard_map/jit(cholesky)/cholesky | solution.py:43
  82.4 9.8 %custom-call.27 = f32[1,128,128]{1,2,0:T(8,128)S(1)} custom-call(f32[1,128,128]{2,1,0:T(8,128)S(1)} %fusion.126), custom_call_target="InvertDiagBlocksLowerTriangular" | custom-call | tf_op jit(solution)/shard_map/jit(_solve_triangular)/triangular_solve | solution.py:44
  92.9 11.7 %cholesky.347 = f32[128,128]{1,0:T(8,128)S(1)} custom-call(f32[128,128]{1,0:T(8,128)S(1)} %fusion.114), custom_call_target="Cholesky" | custom-call | tf_op jit(solution)/shard_map/jit(cholesky)/cholesky | solution.py:45
  106.1 19.3 %custom-call.28 = f32[1,128,128]{1,2,0:T(8,128)S(1)} custom-call(f32[1,128,128]{2,1,0:T(8,128)S(1)} %select_bitcast_fusion.13), custom_call_target="InvertDiagBlocksLowerTriangular" | custom-call | tf_op jit(solution)/shard_map/jit(_solve_triangular)/triangular_solve | solution.py:46
  132.9 11.7 %cholesky.358 = f32[128,128]{1,0:T(8,128)S(1)} custom-call(f32[128,128]{1,0:T(8,128)S(1)} %fusion.112), custom_call_target="Cholesky" | custom-call | tf_op jit(solution)/shard_map/jit(cholesky)/cholesky | solution.py:43
  146.0 9.8 %custom-call.29 = f32[1,128,128]{1,2,0:T(8,128)S(1)} custom-call(f32[1,128,128]{2,1,0:T(8,128)S(1)} %select_bitcast_fusion.12), custom_call_target="InvertDiagBlocksLowerTriangular" | custom-call | tf_op jit(solution)/shard_map/jit(_solve_triangular)/triangular_solve | solution.py:44
  156.5 11.7 %cholesky.369 = f32[128,128]{1,0:T(8,128)S(1)} custom-call(f32[128,128]{1,0:T(8,128)S(1)} %fusion.110), custom_call_target="Cholesky" | custom-call | tf_op jit(solution)/shard_map/jit(cholesky)/cholesky | solution.py:45
  169.7 10.2 %custom-call.30 = f32[1,128,128]{1,2,0:T(8,128)S(1)} custom-call(f32[1,128,128]{2,1,0:T(8,128)S(1)} %select_bitcast_fusion.11), custom_call_target="InvertDiagBlocksLowerTriangular" | custom-call | tf_op jit(solution)/shard_map/jit(_solve_triangular)/triangular_solve | solution.py:46
  183.7 5.3 collective-permute-done.2
  189.5 11.7 %cholesky.380 = f32[128,128]{1,0:T(8,128)S(1)} custom-call(f32[128,128]{1,0:T(8,128)S(1)} %fusion.108), custom_call_target="Cholesky" | custom-call | tf_op jit(solution)/shard_map/jit(cholesky)/cholesky | solution.py:43
  202.6 9.8 %custom-call.31 = f32[1,128,128]{1,2,0:T(8,128)S(1)} custom-call(f32[1,128,128]{2,1,0:T(8,128)S(1)} %select_bitcast_fusion.10), custom_call_target="InvertDiagBlocksLowerTriangular" | custom-call | tf_op jit(solution)/shard_map/jit(_solve_triangular)/triangular_solve | solution.py:44
  213.1 11.7 %cholesky.391 = f32[128,128]{1,0:T(8,128)S(1)} custom-call(f32[128,128]{1,0:T(8,128)S(1)} %fusion.106), custom_call_target="Cholesky" | custom-call | tf_op jit(solution)/shard_map/jit(cholesky)/cholesky | solution.py:45
  226.3 9.9 %custom-call.32 = f32[1,128,128]{1,2,0:T(8,128)S(1)} custom-call(f32[1,128,128]{2,1,0:T(8,128)S(1)} %select_bitcast_fusion.9), custom_call_target="InvertDiagBlocksLowerTriangular" | custom-call | tf_op jit(solution)/shard_map/jit(_solve_triangular)/triangular_solve | solution.py:46
  237.9 3.7 collective-permute-start.3
  241.9 4.9 collective-permute-done.3
  247.3 11.7 %cholesky.402 = f32[128,128]{1,0:T(8,128)S(1)} custom-call(f32[128,128]{1,0:T(8,128)S(1)} %fusion.104), custom_call_target="Cholesky" | custom-call | tf_op jit(solution)/shard_map/jit(cholesky)/cholesky | solution.py:43
  260.4 9.8 %custom-call.33 = f32[1,128,128]{1,2,0:T(8,128)S(1)} custom-call(f32[1,128,128]{2,1,0:T(8,128)S(1)} %fusion.68), custom_call_target="InvertDiagBlocksLowerTriangular" | custom-call | tf_op jit(solution)/shard_map/jit(_solve_triangular)/triangular_solve | solution.py:44
  270.9 11.7 %cholesky.413 = f32[128,128]{1,0:T(8,128)S(1)} custom-call(f32[128,128]{1,0:T(8,128)S(1)} %fusion.102), custom_call_target="Cholesky" | custom-call | tf_op jit(solution)/shard_map/jit(cholesky)/cholesky | solution.py:45
  284.0 10.2 %custom-call.34 = f32[1,128,128]{1,2,0:T(8,128)S(1)} custom-call(f32[1,128,128]{2,1,0:T(8,128)S(1)} %fusion.69), custom_call_target="InvertDiagBlocksLowerTriangular" | custom-call | tf_op jit(solution)/shard_map/jit(_solve_triangular)/triangular_solve | solution.py:46
  295.4 4.3 reduce_sum.37
  300.4 4.7 collective-permute-start.4
  306.3 134.4 %all-gather.7.cloned.1.call-done = f32[32,4,128,256]{3,2,1,0:T(8,128)} async-done(((f32[1,4,128,256]{3,2,1,0:T(8,128)}), f32[32,4,128,256]{3,2,1,0:T(8,128)}) %all-gather.7.cloned.1.call-update) | async-done | bytes 16777232 | tf_op jit(solution)/shard_map/all_gather | solution.py:15
  440.7 6.9 reduce_sum.36
  451.4 5.1 collective-permute-done.5
  456.9 4.4 collective-permute-start.6
  461.3 11.3 %collective-permute-done.6 = f32[128,512]{1,0:T(8,128)S(1)} collective-permute-done((f32[128,512]{1,0:T(8,128)S(1)}, f32[128,512]{1,0:T(8,128)S(1)}, u32[]{:S(2)}, u32[]{:S(2)}) %collective-permute-start.6) | collective-permute-done | bytes 262176 | tf_op jit(solution)/shard_map/ppermute | solution.py:10
  473.0 8.5 collective-permute-start.7
  481.7 11.5 %collective-permute-done.7 = f32[128,512]{1,0:T(8,128)S(1)} collective-permute-done((f32[128,512]{1,0:T(8,128)S(1)}, f32[128,512]{1,0:T(8,128)S(1)}, u32[]{:S(2)}, u32[]{:S(2)}) %collective-permute-start.7) | collective-permute-done | bytes 262176 | tf_op jit(solution)/shard_map/ppermute | solution.py:10
  497.2 11.7 %cholesky.424 = f32[128,128]{1,0:T(8,128)S(1)} custom-call(f32[128,128]{1,0:T(8,128)S(1)} %fusion.91), custom_call_target="Cholesky" | custom-call | tf_op jit(solution)/shard_map/jit(cholesky)/cholesky | solution.py:43
  510.3 9.8 %custom-call.36 = f32[1,128,128]{1,2,0:T(8,128)S(1)} custom-call(f32[1,128,128]{2,1,0:T(8,128)S(1)} %select_bitcast_fusion.7), custom_call_target="InvertDiagBlocksLowerTriangular" | custom-call | tf_op jit(solution)/shard_map/jit(_solve_triangular)/triangular_solve | solution.py:44
  521.0 11.9 %cholesky.435 = f32[128,128]{1,0:T(8,128)S(1)} custom-call(f32[128,128]{1,0:T(8,128)S(1)} %fusion.89), custom_call_target="Cholesky" | custom-call | tf_op jit(solution)/shard_map/jit(cholesky)/cholesky | solution.py:45
  534.4 9.8 %custom-call.45 = f32[1,128,128]{1,2,0:T(8,128)S(1)} custom-call(f32[1,128,128]{2,1,0:T(8,128)S(1)} %select_bitcast_fusion), custom_call_target="InvertDiagBlocksLowerTriangular" | custom-call | tf_op jit(solution)/shard_map/jit(_solve_triangular)/triangular_solve | solution.py:46
  551.6 11.7 %cholesky.446 = f32[128,128]{1,0:T(8,128)S(1)} custom-call(f32[128,128]{1,0:T(8,128)S(1)} %fusion.88), custom_call_target="Cholesky" | custom-call | tf_op jit(solution)/shard_map/jit(cholesky)/cholesky | solution.py:43
  564.7 9.8 %custom-call.37 = f32[1,128,128]{1,2,0:T(8,128)S(1)} custom-call(f32[1,128,128]{2,1,0:T(8,128)S(1)} %select_bitcast_fusion.6), custom_call_target="InvertDiagBlocksLowerTriangular" | custom-call | tf_op jit(solution)/shard_map/jit(_solve_triangular)/triangular_solve | solution.py:44
  575.2 11.7 %cholesky.457 = f32[128,128]{1,0:T(8,128)S(1)} custom-call(f32[128,128]{1,0:T(8,128)S(1)} %fusion.86), custom_call_target="Cholesky" | custom-call | tf_op jit(solution)/shard_map/jit(cholesky)/cholesky | solution.py:45
  588.4 10.2 %custom-call.38 = f32[1,128,128]{1,2,0:T(8,128)S(1)} custom-call(f32[1,128,128]{2,1,0:T(8,128)S(1)} %select_bitcast_fusion.5), custom_call_target="InvertDiagBlocksLowerTriangular" | custom-call | tf_op jit(solution)/shard_map/jit(_solve_triangular)/triangular_solve | solution.py:46
  606.2 11.7 %cholesky.468 = f32[128,128]{1,0:T(8,128)S(1)} custom-call(f32[128,128]{1,0:T(8,128)S(1)} %fusion.84), custom_call_target="Cholesky" | custom-call | tf_op jit(solution)/shard_map/jit(cholesky)/cholesky | solution.py:43
  619.2 9.8 %custom-call.39 = f32[1,128,128]{1,2,0:T(8,128)S(1)} custom-call(f32[1,128,128]{2,1,0:T(8,128)S(1)} %select_bitcast_fusion.4), custom_call_target="InvertDiagBlocksLowerTriangular" | custom-call | tf_op jit(solution)/shard_map/jit(_solve_triangular)/triangular_solve | solution.py:44
  629.7 11.7 %cholesky.479 = f32[128,128]{1,0:T(8,128)S(1)} custom-call(f32[128,128]{1,0:T(8,128)S(1)} %fusion.82), custom_call_target="Cholesky" | custom-call | tf_op jit(solution)/shard_map/jit(cholesky)/cholesky | solution.py:45
  642.9 9.9 %custom-call.40 = f32[1,128,128]{1,2,0:T(8,128)S(1)} custom-call(f32[1,128,128]{2,1,0:T(8,128)S(1)} %select_bitcast_fusion.3), custom_call_target="InvertDiagBlocksLowerTriangular" | custom-call | tf_op jit(solution)/shard_map/jit(_solve_triangular)/triangular_solve | solution.py:46
  661.6 11.7 %cholesky.490 = f32[128,128]{1,0:T(8,128)S(1)} custom-call(f32[128,128]{1,0:T(8,128)S(1)} %fusion.80), custom_call_target="Cholesky" | custom-call | tf_op jit(solution)/shard_map/jit(cholesky)/cholesky | solution.py:43
  674.7 9.8 %custom-call.41 = f32[1,128,128]{1,2,0:T(8,128)S(1)} custom-call(f32[1,128,128]{2,1,0:T(8,128)S(1)} %select_bitcast_fusion.2), custom_call_target="InvertDiagBlocksLowerTriangular" | custom-call | tf_op jit(solution)/shard_map/jit(_solve_triangular)/triangular_solve | solution.py:44
  685.2 11.7 %cholesky.501 = f32[128,128]{1,0:T(8,128)S(1)} custom-call(f32[128,128]{1,0:T(8,128)S(1)} %fusion.78), custom_call_target="Cholesky" | custom-call | tf_op jit(solution)/shard_map/jit(cholesky)/cholesky | solution.py:45
  698.4 10.0 %custom-call.42 = f32[1,128,128]{1,2,0:T(8,128)S(1)} custom-call(f32[1,128,128]{2,1,0:T(8,128)S(1)} %select_bitcast_fusion.1), custom_call_target="InvertDiagBlocksLowerTriangular" | custom-call | tf_op jit(solution)/shard_map/jit(_solve_triangular)/triangular_solve | solution.py:46
  710.0 4.5 collective-permute-start.11
  714.8 4.1 collective-permute-done.11
  719.5 11.7 %cholesky.512 = f32[128,128]{1,0:T(8,128)S(1)} custom-call(f32[128,128]{1,0:T(8,128)S(1)} %fusion.76), custom_call_target="Cholesky" | custom-call | tf_op jit(solution)/shard_map/jit(cholesky)/cholesky | solution.py:43
  732.5 9.8 %custom-call.43 = f32[1,128,128]{1,2,0:T(8,128)S(1)} custom-call(f32[1,128,128]{2,1,0:T(8,128)S(1)} %fusion.70), custom_call_target="InvertDiagBlocksLowerTriangular" | custom-call | tf_op jit(solution)/shard_map/jit(_solve_triangular)/triangular_solve | solution.py:44
  743.0 11.7 %cholesky.523 = f32[128,128]{1,0:T(8,128)S(1)} custom-call(f32[128,128]{1,0:T(8,128)S(1)} %fusion.74), custom_call_target="Cholesky" | custom-call | tf_op jit(solution)/shard_map/jit(cholesky)/cholesky | solution.py:45
  756.1 10.0 %custom-call.44 = f32[1,128,128]{1,2,0:T(8,128)S(1)} custom-call(f32[1,128,128]{2,1,0:T(8,128)S(1)} %fusion.71), custom_call_target="InvertDiagBlocksLowerTriangular" | custom-call | tf_op jit(solution)/shard_map/jit(_solve_triangular)/triangular_solve | solution.py:46
  767.3 4.3 reduce_sum.39
  772.3 5.2 collective-permute-start.12
  778.7 130.0 %all-gather.9.cloned.1.call-done = f32[32,4,128,256]{3,2,1,0:T(8,128)} async-done(((f32[1,4,128,256]{3,2,1,0:T(8,128)}), f32[32,4,128,256]{3,2,1,0:T(8,128)}) %all-gather.9.cloned.1.call-update) | async-done | bytes 16777232 | tf_op jit(solution)/shard_map/all_gather | solution.py:15
  908.7 6.9 reduce_sum.38
  919.3 5.1 collective-permute-done.13
  924.9 4.4 collective-permute-start.14
  929.2 11.3 %collective-permute-done.14 = f32[128,512]{1,0:T(8,128)S(1)} collective-permute-done((f32[128,512]{1,0:T(8,128)S(1)}, f32[128,512]{1,0:T(8,128)S(1)}, u32[]{:S(2)}, u32[]{:S(2)}) %collective-permute-start.14) | collective-permute-done | bytes 262176 | tf_op jit(solution)/shard_map/ppermute | solution.py:10
  941.0 8.5 collective-permute-start.15
  949.6 11.6 %collective-permute-done.15 = f32[128,512]{1,0:T(8,128)S(1)} collective-permute-done((f32[128,512]{1,0:T(8,128)S(1)}, f32[128,512]{1,0:T(8,128)S(1)}, u32[]{:S(2)}, u32[]{:S(2)}) %collective-permute-start.15) | collective-permute-done | bytes 262176 | tf_op jit(solution)/shard_map/ppermute | solution.py:10
  (210 shorter events, 103.1 us)
Async XLA Ops:
  6.5 293.1 %copy-start = (f32[512,512]{1,0:T(8,128)S(1)}, f32[512,512]{1,0:T(8,128)}, u32[]{:S(2)}) copy-start(f32[512,512]{1,0:T(8,128)} %param.6) | copy-start | bytes 3145732
  6.5 288.9 %all-gather.11.cloned.1.call-start = ((), (), s32[]{:S(2)}) async-start(), calls=%async_computation.2 | async-start | bytes 8650752 | tf_op jit(solution)/shard_map/all_gather | solution.py:15
  57.5 383.2 %all-gather.7.cloned.1.call-start = ((), (), s32[]{:S(2)}) async-start(), calls=%async_computation | async-start | bytes 17301504 | tf_op jit(solution)/shard_map/all_gather | solution.py:15
  59.2 9.6 collective-permute-start
  127.0 5.4 collective-permute-start.1
  181.5 7.5 collective-permute-start.2
  237.9 8.9 collective-permute-start.3
  295.3 472.0 %all-gather.13.cloned.1.call-start = ((), (), s32[]{:S(2)}) async-start(), calls=%async_computation.3 | async-start | bytes 8650752 | tf_op jit(solution)/shard_map/all_gather | solution.py:15
  300.4 5.8 collective-permute-start.4
  448.1 8.4 collective-permute-start.5
  456.9 15.7 %collective-permute-start.6 = (f32[128,512]{1,0:T(8,128)S(1)}, f32[128,512]{1,0:T(8,128)S(1)}, u32[]{:S(2)}, u32[]{:S(2)}) collective-permute-start(f32[128,512]{1,0:T(8,128)S(1)} %fusion.4), channel_id=1, source_target_pairs={{0,128},{32,160},{64,192},{96,224},{128,0},{160,32},{192,64},{224,... | collective-permute-start | bytes 786440 | tf_op jit(solution)/shard_map/ppermute | solution.py:10
  473.0 20.2 %collective-permute-start.7 = (f32[128,512]{1,0:T(8,128)S(1)}, f32[128,512]{1,0:T(8,128)S(1)}, u32[]{:S(2)}, u32[]{:S(2)}) collective-permute-start(f32[128,512]{1,0:T(8,128)S(1)} %fusion.8), channel_id=1, source_target_pairs={{0,256},{32,288},{64,320},{96,352},{128,384},{160,416},{192,448},{... | collective-permute-start | bytes 786440 | tf_op jit(solution)/shard_map/ppermute | solution.py:10
  545.3 363.3 %all-gather.9.cloned.1.call-start = ((), (), s32[]{:S(2)}) async-start(), calls=%async_computation.1 | async-start | bytes 17301504 | tf_op jit(solution)/shard_map/all_gather | solution.py:15
  547.0 4.1 collective-permute-start.8
  600.2 5.4 collective-permute-start.9
  654.5 6.6 collective-permute-start.10
  710.0 8.9 collective-permute-start.11
  772.3 6.3 collective-permute-start.12
  916.1 8.4 collective-permute-start.13
  924.9 15.6 %collective-permute-start.14 = (f32[128,512]{1,0:T(8,128)S(1)}, f32[128,512]{1,0:T(8,128)S(1)}, u32[]{:S(2)}, u32[]{:S(2)}) collective-permute-start(f32[128,512]{1,0:T(8,128)S(1)} %fusion.20), channel_id=1, source_target_pairs={{0,128},{32,160},{64,192},{96,224},{128,0},{160,32},{192,64},{224,... | collective-permute-start | bytes 786440 | tf_op jit(solution)/shard_map/ppermute | solution.py:10
  941.0 20.1 %collective-permute-start.15 = (f32[128,512]{1,0:T(8,128)S(1)}, f32[128,512]{1,0:T(8,128)S(1)}, u32[]{:S(2)}, u32[]{:S(2)}) collective-permute-start(f32[128,512]{1,0:T(8,128)S(1)} %fusion.24), channel_id=1, source_target_pairs={{0,256},{32,288},{64,320},{96,352},{128,384},{160,416},{192,448},{... | collective-permute-start | bytes 786440 | tf_op jit(solution)/shard_map/ppermute | solution.py:10
Sparse Core Ops, SparseCore 0:
  57.6 108.1 all-gather.10
  295.5 145.2 all-gather.6
  545.5 97.6 all-gather.12
  767.4 141.2 all-gather.8
